TPU v7x, 32 devices: a whole 2x2x4 slice. The times are simulated.
32 devices in a mesh: dp: 16 (over z, y, core), tensor: 2 (over x).
Axes of the slice: x: 2, y: 2, z: 4, core: 2. Of those that a mesh axis runs over, the one named last changes fastest.
Arguments:
- latents: bfloat16 [16384, 1024], P(('dp', 'tensor')), may hold values from -6 to 6
- inputs: bfloat16 [65536, 1024], P(('dp', 'tensor')), may hold values from -6 to 6
- frames: int32 [128], replicated, may hold values from 4 to 16, as said below
- group_clip: int32 [128], P('dp'), may hold values from 0 to 127, each once
- norm_gain: float32 [4, 1024], replicated, may hold values from 0.5 to 1.5
- norm_bias: float32 [4, 1024], replicated, may hold values from -2 to 2
- cross_q: bfloat16 [1024, 1024], P(None, 'tensor'), may hold values from -0.1875 to 0.1875
- cross_k: bfloat16 [1024, 1024], P(None, 'tensor'), may hold values from -0.1875 to 0.1875
- cross_v: bfloat16 [1024, 1024], P(None, 'tensor'), may hold values from -0.1875 to 0.1875
- cross_o: bfloat16 [1024, 1024], P('tensor'), may hold values from -1 to 1
- self_q: bfloat16 [1024, 1024], P(None, 'tensor'), may hold values from -0.1875 to 0.1875
- self_k: bfloat16 [1024, 1024], P(None, 'tensor'), may hold values from -0.1875 to 0.1875
- self_v: bfloat16 [1024, 1024], P(None, 'tensor'), may hold values from -0.1875 to 0.1875
- self_o: bfloat16 [1024, 1024], P('tensor'), may hold values from -0.75 to 0.75
- mlp_up: bfloat16 [1024, 4096], P(None, 'tensor'), may hold values from -0.1875 to 0.1875
- up_bias: bfloat16 [4096], P('tensor'), may hold values from -3 to 3
- mlp_down: bfloat16 [4096, 1024], P('tensor'), may hold values from -0.09375 to 0.09375
- out_bias: float32 [3, 1024], replicated, may hold values from -2 to 2
- cotangent: bfloat16 [16384, 1024], P(('dp', 'tensor')), may hold values from -6 to 6
Outputs:
- result: bfloat16 [16384, 1024], P(('dp', 'tensor'))
- d_latents: float32 [16384, 1024], P(('dp', 'tensor'))
- d_inputs: float32 [65536, 1024], P(('dp', 'tensor'))
- d_norm_gain: float32 [4, 1024], replicated
- d_norm_bias: float32 [4, 1024], replicated
- d_out_bias: float32 [3, 1024], replicated
- d_cross_q: float32 [1024, 1024], P(None, 'tensor')
- d_cross_k: float32 [1024, 1024], P(None, 'tensor')
- d_cross_v: float32 [1024, 1024], P(None, 'tensor')
- d_cross_o: float32 [1024, 1024], P('tensor')
- d_self_q: float32 [1024, 1024], P(None, 'tensor')
- d_self_k: float32 [1024, 1024], P(None, 'tensor')
- d_self_v: float32 [1024, 1024], P(None, 'tensor')
- d_self_o: float32 [1024, 1024], P('tensor')
- d_mlp_up: float32 [1024, 4096], P(None, 'tensor')
- d_up_bias: float32 [4096], P('tensor')
- d_mlp_down: float32 [4096, 1024], P('tensor')
Inputs may be any that keep to these rules, and one draw needn't show every extreme that they name: Each clip has 4 or 16 frames, and both counts occur. `group_clip`: every clip index belongs to exactly one group.
All inputs are finite; a program needn't handle non-finite values.
Results may differ from a plain program's by a relative error of at most 0.03.
Values may be sent and summed in bfloat16 or wider, within the bound.
A program may use at most 256 MiB of HBM per device.

v0:
```python
import jax
import jax.numpy as jnp
from jax import lax
from jax.sharding import PartitionSpec as P

HS = 128
LAT = 128
FRAME_ROWS = 32
EPSILON = 1e-05
NEG_LARGE = -1e30
GELU_COEF = 0.7978845608028654
GELU_CUBE = 0.044715


def layer_norm(values, gain, shift):
    average = jnp.mean(values, axis=-1, keepdims=True)
    centered = values - average
    variance = jnp.mean(centered * centered, axis=-1, keepdims=True)
    return centered * lax.rsqrt(variance + EPSILON) * gain + shift


def gelu_tanh(values):
    inner = GELU_COEF * (values + GELU_CUBE * values * values * values)
    return 0.5 * values * (1.0 + jnp.tanh(inner))


def gelu_slope(values):
    squared = values * values
    hyperbolic = jnp.tanh(GELU_COEF * (values + GELU_CUBE * squared * values))
    return 0.5 * (1.0 + hyperbolic) + 0.5 * values * (1.0 - hyperbolic * hyperbolic) * GELU_COEF * (
        1.0 + 3.0 * GELU_CUBE * squared
    )


def matmul(left, right):
    return jnp.dot(left, right, preferred_element_type=jnp.float32)


def gram_left(left, right):
    return lax.dot_general(
        left, right, (((0,), (0,)), ((), ())), preferred_element_type=jnp.float32
    )


def times_transposed(left, right):
    return lax.dot_general(
        left, right, (((1,), (1,)), ((), ())), preferred_element_type=jnp.float32
    )


def block_size(groups):
    chosen = 1
    for candidate in (4, 3, 2):
        if chosen == 1 and groups % candidate == 0:
            chosen = candidate
    return chosen


def split_blocks(array, groups, head_size):
    block = block_size(groups)
    rows = array.shape[0] // groups
    heads = array.shape[1] // head_size
    return array.reshape(groups // block, block, rows, heads, head_size)


def masked_scores(query_block, key_block, length_block, head_size):
    key_count = key_block.shape[1]
    scores = jnp.einsum(
        "gqhd,gkhd->ghqk", query_block, key_block, preferred_element_type=jnp.float32
    ) * head_size ** (-0.5)
    positions = lax.broadcasted_iota(jnp.int32, (1, 1, 1, key_count), 3)
    return jnp.where(positions < length_block[:, None, None, None], scores, NEG_LARGE)


def attend_forward(queries, key_vecs, value_vecs, lengths, head_size):
    groups = lengths.shape[0]
    block = block_size(groups)
    pieces = (
        split_blocks(queries, groups, head_size),
        split_blocks(key_vecs, groups, head_size),
        split_blocks(value_vecs, groups, head_size),
        lengths.reshape(groups // block, block),
    )

    def one_block(piece):
        query_block, key_block, value_block, length_block = piece
        scores = masked_scores(query_block, key_block, length_block, head_size)
        row_max = jnp.max(scores, axis=-1, keepdims=True)
        exponent = jnp.exp(scores - row_max)
        row_total = jnp.sum(exponent, axis=-1, keepdims=True)
        probability = (exponent / row_total).astype(jnp.bfloat16)
        mixed = jnp.einsum(
            "ghqk,gkhd->gqhd", probability, value_block, preferred_element_type=jnp.float32
        )
        return (mixed.astype(jnp.bfloat16), (row_max + jnp.log(row_total))[..., 0])

    mixed, log_total = lax.map(one_block, pieces)
    return (mixed.reshape(queries.shape), log_total)


def attend_backward(queries, key_vecs, value_vecs, grad_mixed, log_total, lengths, head_size):
    groups = lengths.shape[0]
    block = block_size(groups)
    pieces = (
        split_blocks(queries, groups, head_size),
        split_blocks(key_vecs, groups, head_size),
        split_blocks(value_vecs, groups, head_size),
        split_blocks(grad_mixed, groups, head_size),
        log_total,
        lengths.reshape(groups // block, block),
    )
    scale_factor = head_size ** (-0.5)

    def one_block(piece):
        query_block, key_block, value_block, grad_block, total_block, length_block = piece
        scores = masked_scores(query_block, key_block, length_block, head_size)
        probability = jnp.exp(scores - total_block[..., None])
        grad_prob = jnp.einsum(
            "gqhd,gkhd->ghqk", grad_block, value_block, preferred_element_type=jnp.float32
        )
        inner = jnp.sum(probability * grad_prob, axis=-1, keepdims=True)
        grad_score = (probability * (grad_prob - inner)).astype(jnp.bfloat16)
        grad_query = (
            jnp.einsum("ghqk,gkhd->gqhd", grad_score, key_block, preferred_element_type=jnp.float32)
            * scale_factor
        )
        grad_key = (
            jnp.einsum(
                "ghqk,gqhd->gkhd", grad_score, query_block, preferred_element_type=jnp.float32
            )
            * scale_factor
        )
        grad_value = jnp.einsum(
            "ghqk,gqhd->gkhd",
            probability.astype(jnp.bfloat16),
            grad_block,
            preferred_element_type=jnp.float32,
        )
        return (
            grad_query.astype(jnp.bfloat16),
            grad_key.astype(jnp.bfloat16),
            grad_value.astype(jnp.bfloat16),
        )

    grad_query, grad_key, grad_value = lax.map(one_block, pieces)
    return (
        grad_query.reshape(queries.shape),
        grad_key.reshape(key_vecs.shape),
        grad_value.reshape(value_vecs.shape),
    )


def gather_rows(normed):
    return lax.all_gather(normed, "tensor", axis=0, tiled=True)


def gather_grads(grads):
    return lax.all_gather(grads, "tensor", axis=0, tiled=True)


def branch_sum(mixed, weight, own_rows):

    def term(begin_row, row_count):
        return matmul(mixed, weight)

    return lax.psum_scatter(
        term(jnp.int32(0), lax.axis_size("tensor") * own_rows),
        "tensor",
        scatter_dimension=0,
        tiled=True,
    )


def back_rows(term, own_rows):
    return lax.psum_scatter(
        term(jnp.int32(0), own_rows * lax.axis_size("tensor")).astype(jnp.bfloat16),
        "tensor",
        scatter_dimension=0,
        tiled=True,
    ).astype(jnp.float32)


def back_inputs(term, own_rows):
    return lax.psum_scatter(
        term(jnp.int32(0), own_rows * lax.axis_size("tensor")).astype(jnp.bfloat16),
        "tensor",
        scatter_dimension=0,
        tiled=True,
    ).astype(jnp.float32)


def shards(
    latents,
    inputs,
    frames,
    group_clip,
    norm_gain,
    norm_bias,
    cross_q,
    cross_k,
    cross_v,
    cross_o,
    self_q,
    self_k,
    self_v,
    self_o,
    mlp_up,
    up_bias,
    mlp_down,
    out_bias,
    cotangent,
):
    head_size = HS
    own_rows = latents.shape[0]
    own_inputs = inputs.shape[0]
    stream = latents.astype(jnp.float32)
    source = inputs.astype(jnp.float32)
    lat_normed = layer_norm(stream, norm_gain[0], norm_bias[0]).astype(jnp.bfloat16)
    in_normed = layer_norm(source, norm_gain[1], norm_bias[1]).astype(jnp.bfloat16)
    local_set = (
        cross_q,
        cross_k,
        cross_v,
        cross_o,
        self_q,
        self_k,
        self_v,
        self_o,
        mlp_up,
        up_bias,
        mlp_down,
    )
    rows_cross, rows_input = (
        lax.all_gather(lat_normed, "tensor", axis=0, tiled=True),
        lax.all_gather(in_normed, "tensor", axis=0, tiled=True),
    )
    (
        w_cross_q,
        w_cross_k,
        w_cross_v,
        w_cross_o,
        w_self_q,
        w_self_k,
        w_self_v,
        w_self_o,
        w_up,
        b_up,
        w_down,
    ) = local_set
    matches = group_clip[:, None] == lax.broadcasted_iota(jnp.int32, (1, frames.shape[0]), 1)
    lengths = jnp.sum(jnp.where(matches, frames[None, :], 0), axis=1) * FRAME_ROWS
    full_lengths = jnp.full(lengths.shape, LAT, jnp.int32)
    cross_query = matmul(rows_cross, w_cross_q).astype(jnp.bfloat16)
    cross_keys = matmul(rows_input, w_cross_k).astype(jnp.bfloat16)
    cross_values = matmul(rows_input, w_cross_v).astype(jnp.bfloat16)
    cross_mixed, cross_total = attend_forward(
        cross_query, cross_keys, cross_values, lengths, head_size
    )
    stream1 = stream + branch_sum(cross_mixed, w_cross_o, own_rows) + out_bias[0]
    self_normed = layer_norm(stream1, norm_gain[2], norm_bias[2]).astype(jnp.bfloat16)
    rows_self = gather_rows(self_normed)
    self_query = matmul(rows_self, w_self_q).astype(jnp.bfloat16)
    self_keys = matmul(rows_self, w_self_k).astype(jnp.bfloat16)
    self_values = matmul(rows_self, w_self_v).astype(jnp.bfloat16)
    self_mixed, self_total = attend_forward(
        self_query, self_keys, self_values, full_lengths, head_size
    )
    stream2 = stream1 + branch_sum(self_mixed, w_self_o, own_rows) + out_bias[1]
    mlp_normed = layer_norm(stream2, norm_gain[3], norm_bias[3]).astype(jnp.bfloat16)
    rows_mlp = gather_rows(mlp_normed)
    pre_act = matmul(rows_mlp, w_up) + b_up.astype(jnp.float32)
    hidden = gelu_tanh(pre_act).astype(jnp.bfloat16)
    stream3 = stream2 + branch_sum(hidden, w_down, own_rows) + out_bias[2]
    result = stream3.astype(jnp.bfloat16)
    grad3 = cotangent.astype(jnp.float32)
    rows_grad3 = gather_grads(grad3.astype(jnp.bfloat16))
    d_down = gram_left(hidden, rows_grad3)
    d_pre = (times_transposed(rows_grad3, w_down) * gelu_slope(pre_act)).astype(jnp.bfloat16)
    d_upb = jnp.sum(d_pre.astype(jnp.float32), axis=0)
    d_up = gram_left(rows_mlp, d_pre)
    d_mlp_rows = back_rows(lambda begin_row, row_count: times_transposed(d_pre, w_up), own_rows)
    ln_value, ln_pull = jax.vjp(layer_norm, stream2, norm_gain[3], norm_bias[3])
    d_stream2, gain_three, shift_three = ln_pull(d_mlp_rows)
    grad2 = grad3 + d_stream2
    rows_grad2 = gather_grads(grad2.astype(jnp.bfloat16))
    self_query = matmul(rows_self, w_self_q).astype(jnp.bfloat16)
    self_keys = matmul(rows_self, w_self_k).astype(jnp.bfloat16)
    self_values = matmul(rows_self, w_self_v).astype(jnp.bfloat16)
    self_mixed, self_total = attend_forward(
        self_query, self_keys, self_values, full_lengths, head_size
    )
    d_self_o = gram_left(self_mixed, rows_grad2)
    d_self_mixed = times_transposed(rows_grad2, w_self_o).astype(jnp.bfloat16)
    d_self_query, d_self_keys, d_self_values = attend_backward(
        self_query, self_keys, self_values, d_self_mixed, self_total, full_lengths, head_size
    )
    d_self_q = gram_left(rows_self, d_self_query)
    d_self_k = gram_left(rows_self, d_self_keys)
    d_self_v = gram_left(rows_self, d_self_values)

    def self_term(begin_row, row_count):
        return (
            times_transposed(d_self_query, w_self_q)
            + times_transposed(d_self_keys, w_self_k)
            + times_transposed(d_self_values, w_self_v)
        )

    d_self_rows = back_rows(self_term, own_rows)
    ln_value, ln_pull = jax.vjp(layer_norm, stream1, norm_gain[2], norm_bias[2])
    d_stream1, gain_two, shift_two = ln_pull(d_self_rows)
    grad1 = grad2 + d_stream1
    rows_grad1 = gather_grads(grad1.astype(jnp.bfloat16))
    d_cross_o = gram_left(cross_mixed, rows_grad1)
    d_cross_mixed = times_transposed(rows_grad1, w_cross_o).astype(jnp.bfloat16)
    d_cross_query, d_cross_keys, d_cross_values = attend_backward(
        cross_query, cross_keys, cross_values, d_cross_mixed, cross_total, lengths, head_size
    )
    d_cross_q = gram_left(rows_cross, d_cross_query)
    d_cross_k = gram_left(rows_input, d_cross_keys)
    d_cross_v = gram_left(rows_input, d_cross_values)
    d_lat_rows = back_rows(
        lambda begin_row, row_count: times_transposed(d_cross_query, w_cross_q), own_rows
    )

    def input_term(begin_row, row_count):
        return times_transposed(d_cross_keys, w_cross_k) + times_transposed(
            d_cross_values, w_cross_v
        )

    d_in_rows = back_inputs(input_term, own_inputs)
    ln_value, ln_pull = jax.vjp(layer_norm, stream, norm_gain[0], norm_bias[0])
    d_stream0, gain_zero, shift_zero = ln_pull(d_lat_rows)
    d_latents = grad1 + d_stream0
    ln_value, ln_pull = jax.vjp(layer_norm, source, norm_gain[1], norm_bias[1])
    d_inputs, gain_one, shift_one = ln_pull(d_in_rows)
    gain_grads = jnp.stack([gain_zero, gain_one, gain_two, gain_three])
    shift_grads = jnp.stack([shift_zero, shift_one, shift_two, shift_three])
    bias_grads = jnp.stack([jnp.sum(grad1, axis=0), jnp.sum(grad2, axis=0), jnp.sum(grad3, axis=0)])
    gain_grads, shift_grads, bias_grads = lax.psum(
        (gain_grads, shift_grads, bias_grads), ("dp", "tensor")
    )
    (
        d_cross_q,
        d_cross_k,
        d_cross_v,
        d_cross_o,
        d_self_q,
        d_self_k,
        d_self_v,
        d_self_o,
        d_up,
        d_upb,
        d_down,
    ) = (
        lax.psum(d_cross_q.astype(jnp.bfloat16), "dp").astype(jnp.float32),
        lax.psum(d_cross_k.astype(jnp.bfloat16), "dp").astype(jnp.float32),
        lax.psum(d_cross_v.astype(jnp.bfloat16), "dp").astype(jnp.float32),
        lax.psum(d_cross_o.astype(jnp.bfloat16), "dp").astype(jnp.float32),
        lax.psum(d_self_q.astype(jnp.bfloat16), "dp").astype(jnp.float32),
        lax.psum(d_self_k.astype(jnp.bfloat16), "dp").astype(jnp.float32),
        lax.psum(d_self_v.astype(jnp.bfloat16), "dp").astype(jnp.float32),
        lax.psum(d_self_o.astype(jnp.bfloat16), "dp").astype(jnp.float32),
        lax.psum(d_up.astype(jnp.bfloat16), "dp").astype(jnp.float32),
        lax.psum(d_upb.astype(jnp.bfloat16), "dp").astype(jnp.float32),
        lax.psum(d_down.astype(jnp.bfloat16), "dp").astype(jnp.float32),
    )
    return (
        result,
        d_latents,
        d_inputs,
        gain_grads,
        shift_grads,
        bias_grads,
        d_cross_q,
        d_cross_k,
        d_cross_v,
        d_cross_o,
        d_self_q,
        d_self_k,
        d_self_v,
        d_self_o,
        d_up,
        d_upb,
        d_down,
    )


def solution(mesh):
    in_specs = (
        P(("dp", "tensor"), None),
        P(("dp", "tensor"), None),
        P(),
        P("dp"),
        P(),
        P(),
        P(None, "tensor"),
        P(None, "tensor"),
        P(None, "tensor"),
        P("tensor", None),
        P(None, "tensor"),
        P(None, "tensor"),
        P(None, "tensor"),
        P("tensor", None),
        P(None, "tensor"),
        P("tensor"),
        P("tensor", None),
        P(),
        P(("dp", "tensor"), None),
    )
    out_specs = (
        P(("dp", "tensor"), None),
        P(("dp", "tensor"), None),
        P(("dp", "tensor"), None),
        P(),
        P(),
        P(),
        P(None, "tensor"),
        P(None, "tensor"),
        P(None, "tensor"),
        P("tensor", None),
        P(None, "tensor"),
        P(None, "tensor"),
        P(None, "tensor"),
        P("tensor", None),
        P(None, "tensor"),
        P("tensor"),
        P("tensor", None),
    )
    return jax.shard_map(shards, mesh=mesh, in_specs=in_specs, out_specs=out_specs, check_vma=False)
```

profile of v0, /device:TPU:0, one launch (start us, length us, event | category | flops | bytes accessed | tf_op | source)
XLA Modules:
  0.0 1340.8 jit_solution(18422580686185604196)
XLA Ops:
  24.9 26.5 %all-gather.10.cloned.1.call-done = bf16[1024,1024]{1,0:T(8,128)(2,1)} async-done(((bf16[512,1024]{1,0:T(8,128)(2,1)}), bf16[1024,1024]{1,0:T(8,128)(2,1)}) %all-gather.10.cloned.1.call-update) | async-done | bytes 2097168 | tf_op jit(solution)/shard_map/all_gather | solution.py:234
  56.0 101.6 %all-gather.8.cloned.1.call-done = bf16[4096,1024]{1,0:T(8,128)(2,1)} async-done(((bf16[2048,1024]{1,0:T(8,128)(2,1)}), bf16[4096,1024]{1,0:T(8,128)(2,1)}) %all-gather.8.cloned.1.call-update) | async-done | bytes 8388624 | tf_op jit(solution)/shard_map/all_gather | solution.py:235
  157.6 9.4 convolution_convert_fusion.3
  179.3 9.4 convolution_convert_fusion.4
  196.8 24.9 %while.62 = (s32[]{:T(128)}, bf16[2,4,128,4,128]{4,3,2,1,0:T(4,128)(2,1)}, f32[2,4,4,128]{3,2,1,0:T(4,128)S(1)}, bf16[2,4,512,4,128]{4,3,2,1,0:T(4,128)(2,1)}, s...) while((s32[]{:T(128)}, ...), condition=%wide.region_8.9_spmd, body=%wide.region_5.8_spmd.sunk | while | flops 549715968 | bytes 45163760 | solution.py:97
  227.2 53.8 %reduce-scatter.8.cloned.1.call-done = f32[512,1024]{1,0:T(8,128)} async-done(((f32[1024,1024]{1,0:T(8,128)}), f32[512,1024]{1,0:T(8,128)}) %reduce-scatter.8.cloned.1.call-update) | async-done | bytes 2097168 | tf_op jit(solution)/shard_map/reduce_scatter | solution.py:166
  285.1 33.2 %all-gather.12.cloned.1.call-done = bf16[1024,1024]{1,0:T(8,128)(2,1)} async-done(((bf16[512,1024]{1,0:T(8,128)(2,1)}), bf16[1024,1024]{1,0:T(8,128)(2,1)}) %all-gather.12.cloned.1.call-update) | async-done | bytes 2097168 | tf_op jit(solution)/shard_map/all_gather | solution.py:154
  345.4 18.6 %while.63 = (s32[]{:T(128)}, bf16[2,4,128,4,128]{4,3,2,1,0:T(4,128)(2,1)}, bf16[2,4,128,4,128]{2,4,3,1,0:T(8,128)(2,1)}, bf16[2,4,128,4,128]{4,2,3,1,0:T(8,128)(...) while((s32[]{:T(128)}, bf16[2,4,128,4,128]{4,3,2,1,0:T(4,128)(2,1)}, ...), condition=%wide.region_15.16_spmd, body=%wide.region_12.15_spmd.sunk | while | flops 136053376 | bytes 6309973 | solution.py:97
  368.9 54.5 %reduce-scatter.10.cloned.1.call-done = f32[512,1024]{1,0:T(8,128)} async-done(((f32[1024,1024]{1,0:T(8,128)}), f32[512,1024]{1,0:T(8,128)}) %reduce-scatter.10.cloned.1.call-update) | async-done | bytes 2097168 | tf_op jit(solution)/shard_map/reduce_scatter | solution.py:166
  429.3 32.0 %all-gather.14.cloned.1.call-done = bf16[1024,1024]{1,0:T(8,128)(2,1)} async-done(((bf16[512,1024]{1,0:T(8,128)(2,1)}), bf16[1024,1024]{1,0:T(8,128)(2,1)}) %all-gather.14.cloned.1.call-update) | async-done | bytes 2097168 | tf_op jit(solution)/shard_map/all_gather | solution.py:154
  461.3 10.9 fusion.228
  472.1 23.8 %all-gather.16.cloned.1.call-done = bf16[1024,1024]{1,0:T(8,128)(2,1)} async-done(((bf16[512,1024]{1,0:T(8,128)(2,1)}), bf16[1024,1024]{1,0:T(8,128)(2,1)}) %all-gather.16.cloned.1.call-update) | async-done | bytes 2097168 | tf_op jit(solution)/shard_map/all_gather | solution.py:158
  495.9 13.1 fusion.227
  517.0 11.8 fusion.211
  528.9 19.9 %reduce-scatter.14.cloned.1.call-done = bf16[512,1024]{1,0:T(8,128)(2,1)} async-done(((bf16[1024,1024]{1,0:T(8,128)(2,1)}), bf16[512,1024]{1,0:T(8,128)(2,1)}) %reduce-scatter.14.cloned.1.call-update) | async-done | bytes 1048592 | tf_op jit(solution)/shard_map/reduce_scatter | solution.py:175
  551.5 54.1 %reduce-scatter.12.cloned.1.call-done = f32[512,1024]{1,0:T(8,128)} async-done(((f32[1024,1024]{1,0:T(8,128)}), f32[512,1024]{1,0:T(8,128)}) %reduce-scatter.12.cloned.1.call-update) | async-done | bytes 2097168 | tf_op jit(solution)/shard_map/reduce_scatter | solution.py:166
  614.3 8.9 while.64
  623.2 22.8 %all-gather.18.cloned.1.call-done = bf16[1024,1024]{1,0:T(8,128)(2,1)} async-done(((bf16[512,1024]{1,0:T(8,128)(2,1)}), bf16[1024,1024]{1,0:T(8,128)(2,1)}) %all-gather.18.cloned.1.call-update) | async-done | bytes 2097168 | tf_op jit(solution)/shard_map/all_gather | solution.py:158
  656.0 22.7 %while.65 = (s32[]{:T(128)}, bf16[2,4,128,4,128]{4,3,2,1,0:T(4,128)(2,1)}, bf16[2,4,128,4,128]{4,3,2,1,0:T(4,128)(2,1)}, bf16[2,4,128,4,128]{4,3,2,1,0:T(4,128)(...) while((s32[]{:T(128)}, ...), condition=%wide.region_29.30_spmd, body=%wide.region_27.29_spmd.sunk | while | flops 339212800 | bytes 40413460 | solution.py:145
  686.3 12.6 convolution_convert_fusion.5
  698.9 19.1 %reduce-scatter.16.cloned.1.call-done = bf16[512,1024]{1,0:T(8,128)(2,1)} async-done(((bf16[1024,1024]{1,0:T(8,128)(2,1)}), bf16[512,1024]{1,0:T(8,128)(2,1)}) %reduce-scatter.16.cloned.1.call-update) | async-done | bytes 1048592 | tf_op jit(solution)/shard_map/reduce_scatter | solution.py:175
  728.3 9.6 convolution_convert_fusion.6
  744.7 16.3 %all-gather.20.cloned.1.call-done = bf16[1024,1024]{1,0:T(8,128)(2,1)} async-done(((bf16[512,1024]{1,0:T(8,128)(2,1)}), bf16[1024,1024]{1,0:T(8,128)(2,1)}) %all-gather.20.cloned.1.call-update) | async-done | bytes 2097168 | tf_op jit(solution)/shard_map/all_gather | solution.py:158
  765.6 64.0 %while.66 = (s32[]{:T(128)}, bf16[2,4,128,4,128]{4,3,2,1,0:T(4,128)(2,1)}, bf16[2,4,512,4,128]{4,3,2,1,0:T(4,128)(2,1)}, bf16[2,4,512,4,128]{4,3,2,1,0:T(4,128)(...) while((s32[]{:T(128)}, ...), condition=%wide.region_35.36_spmd, body=%wide.region_33.35_spmd.sunk | while | flops 1361575936 | bytes 150537648 | solution.py:145
  842.7 9.1 fusion.171
  857.4 10.5 fusion.142
  868.0 11.4 add_convert_fusion
  880.0 35.8 %psum.110 = bf16[2048]{0:T(1024)(128)(2,1)S(1)} all-reduce(bf16[2048]{0:T(1024)(128)(2,1)S(1)} %copy-done.87), channel_id=1, replica_groups=mesh['dp'=16,'tensor'=2] {'dp'}, use_global_device_ids=true, to_apply=%region_66.67 | all-reduce | flops 2048 | bytes 8192 | tf_op jit(solution)/shard_map/psum | solution.py:364
  923.2 249.8 %all-reduce.4.cloned.1.call-done = (bf16[1024,512]{1,0:T(8,128)(2,1)}, bf16[1024,512]{1,0:T(8,128)(2,1)}, bf16[1024,512]{1,0:T(8,128)(2,1)}, bf16[512,1024]{1,0:...) async-done(((bf16[1024,512]{1,0:T(8,128)(2,1)}, ...) | async-done | bytes 16777232 | tf_op jit(solution)/shard_map/psum | solution.py:355
  1197.4 77.4 %reduce-scatter.20.cloned.1.call-done = bf16[2048,1024]{1,0:T(8,128)(2,1)} async-done(((bf16[4096,1024]{1,0:T(8,128)(2,1)}), bf16[2048,1024]{1,0:T(8,128)(2,1)}) %reduce-scatter.20.cloned.1.call-update) | async-done | bytes 4194320 | tf_op jit(solution)/shard_map/reduce_scatter | solution.py:184
  1286.3 40.3 %all-reduce = (f32[4,1024]{1,0:T(4,128)}, f32[4,1024]{1,0:T(4,128)}, f32[3,1024]{1,0:T(4,128)}) all-reduce(f32[4,1024]{1,0:T(4,128)S(1)} %get-tuple-element.481, f32[4,1024]{1,0:T(4,128)S(1)} %get-tuple-element.482, f32[3,1024]{1,0:T(4,128)S(1)} %pad_maximum_fusion.2), channel_id=1, replica_groups=mesh['dp'=16,'tensor'=2] {'dp','tensor'}, use_global_device_ids=true, to_apply=%region_46.47 | all-reduce | flops 11264 | bytes 90112 | tf_op jit(solution)/shard_map/psum | solution.py:339
  1326.6 7.2 fusion.135
  (480 shorter events, 349.2 us)
Async XLA Ops:
  7.2 150.5 %copy-start = (bf16[1024,512]{1,0:T(8,128)(2,1)S(1)}, bf16[1024,512]{1,0:T(8,128)(2,1)}, u32[]{:S(2)}) copy-start(bf16[1024,512]{1,0:T(8,128)(2,1)} %param.36) | copy-start | bytes 3145732
  7.2 44.3 %all-gather.10.cloned.1.call-start = ((), (), s32[]{:S(2)}) async-start(), calls=%async_computation.8 | async-start | bytes 3145728 | tf_op jit(solution)/shard_map/all_gather | solution.py:234
  11.9 271.8 %copy-start.60 = (f32[1,1024]{1,0:T(1,128)}, f32[1,1024]{1,0:T(1,128)S(1)}, u32[]{:S(2)}) copy-start(f32[1,1024]{1,0:T(1,128)S(1)} %get-tuple-element.474) | copy-start | bytes 12292
  15.5 142.1 %all-gather.8.cloned.1.call-start = ((), (), s32[]{:S(2)}) async-start(), calls=%async_computation.7 | async-start | bytes 12582912 | tf_op jit(solution)/shard_map/all_gather | solution.py:235
  24.0 257.0 %reduce-scatter.8.cloned.1.call-start = ((), (), s32[]{:S(2)}) async-start(), calls=%async_computation.9 | async-start | bytes 6291456 | tf_op jit(solution)/shard_map/reduce_scatter | solution.py:166
  226.5 91.8 %all-gather.12.cloned.1.call-start = ((), (), s32[]{:S(2)}) async-start(), calls=%async_computation.10 | async-start | bytes 3145728 | tf_op jit(solution)/shard_map/all_gather | solution.py:154
  283.3 140.1 %copy-start.8 = (f32[512,1024]{1,0:T(8,128)}, f32[512,1024]{1,0:T(8,128)S(1)}, u32[]{:S(2)}) copy-start(f32[512,1024]{1,0:T(8,128)S(1)} %get-tuple-element.451) | copy-start | bytes 6291460
  283.3 39.1 %copy-start.66 = (f32[512]{0:T(512)}, f32[512]{0:T(512)S(1)}, u32[]{:S(2)}) copy-start(f32[512]{0:T(512)S(1)} %broadcast_multiply_fusion.2) | copy-start | bytes 6148
  283.6 38.8 %copy-start.76 = (f32[512]{0:T(512)}, f32[512]{0:T(512)S(1)}, u32[]{:S(2)}) copy-start(f32[512]{0:T(512)S(1)} %multiply_reduce_fusion.3) | copy-start | bytes 6148
  283.7 38.7 %copy-start.70 = (f32[512]{0:T(512)}, f32[512]{0:T(512)S(1)}, u32[]{:S(2)}) copy-start(f32[512]{0:T(512)S(1)} %fusion.205) | copy-start | bytes 6148
  285.1 138.3 %reduce-scatter.10.cloned.1.call-start = ((), (), s32[]{:S(2)}) async-start(), calls=%async_computation.11 | async-start | bytes 6291456 | tf_op jit(solution)/shard_map/reduce_scatter | solution.py:166
  368.9 92.4 %all-gather.14.cloned.1.call-start = ((), (), s32[]{:S(2)}) async-start(), calls=%async_computation.12 | async-start | bytes 3145728 | tf_op jit(solution)/shard_map/all_gather | solution.py:154
  428.0 67.9 %all-gather.16.cloned.1.call-start = ((), (), s32[]{:S(2)}) async-start(), calls=%async_computation.14 | async-start | bytes 3145728 | tf_op jit(solution)/shard_map/all_gather | solution.py:158
  428.8 120.1 %reduce-scatter.14.cloned.1.call-start = ((), (), s32[]{:S(2)}) async-start(), calls=%async_computation.15 | async-start | bytes 3145728 | tf_op jit(solution)/shard_map/reduce_scatter | solution.py:175
  516.8 88.8 %reduce-scatter.12.cloned.1.call-start = ((), (), s32[]{:S(2)}) async-start(), calls=%async_computation.13 | async-start | bytes 6291456 | tf_op jit(solution)/shard_map/reduce_scatter | solution.py:166
  528.8 117.1 %all-gather.18.cloned.1.call-start = ((), (), s32[]{:S(2)}) async-start(), calls=%async_computation.16 | async-start | bytes 3145728 | tf_op jit(solution)/shard_map/all_gather | solution.py:158
  612.7 105.3 %reduce-scatter.16.cloned.1.call-start = ((), (), s32[]{:S(2)}) async-start(), calls=%async_computation.17 | async-start | bytes 3145728 | tf_op jit(solution)/shard_map/reduce_scatter | solution.py:175
  685.9 75.1 %all-gather.20.cloned.1.call-start = ((), (), s32[]{:S(2)}) async-start(), calls=%async_computation.18 | async-start | bytes 3145728 | tf_op jit(solution)/shard_map/all_gather | solution.py:158
  727.8 188.8 %reduce-scatter.18.cloned.1.call-start = ((), (), s32[]{:S(2)}) async-start(), calls=%async_computation.19 | async-start | bytes 3145728 | tf_op jit(solution)/shard_map/reduce_scatter | solution.py:175
  833.9 339.1 %all-reduce.4.cloned.1.call-start = ((), (), s32[]{:S(2)}) async-start(), calls=%async_computation.21 | async-start | bytes 33554432 | tf_op jit(solution)/shard_map/psum | solution.py:355
  857.4 417.4 %reduce-scatter.20.cloned.1.call-start = ((), (), s32[]{:S(2)}) async-start(), calls=%async_computation.20 | async-start | bytes 12582912 | tf_op jit(solution)/shard_map/reduce_scatter | solution.py:184
  879.3 37.1 %copy-start.82 = (f32[1024]{0:T(1024)S(1)}, f32[1024]{0:T(1024)}, u32[]{:S(2)}) copy-start(f32[1024]{0:T(1024)} %get-tuple-element.444) | copy-start | bytes 12292
  879.3 37.1 %copy-start.83 = (f32[1024]{0:T(1024)S(1)}, f32[1024]{0:T(1024)}, u32[]{:S(2)}) copy-start(f32[1024]{0:T(1024)} %get-tuple-element.350) | copy-start | bytes 12292
  879.4 37.2 %copy-start.16 = (bf16[512,1024]{1,0:T(8,128)(2,1)S(1)}, bf16[512,1024]{1,0:T(8,128)(2,1)}, u32[]{:S(2)}) copy-start(bf16[512,1024]{1,0:T(8,128)(2,1)} %param.29) | copy-start | bytes 3145732
  879.4 37.2 %copy-start.63 = (f32[1,1024]{1,0:T(1,128)S(1)}, f32[1,1024]{1,0:T(1,128)}, u32[]{:S(2)}) copy-start(f32[1,1024]{1,0:T(1,128)} %copy-done.62) | copy-start | bytes 12292
  879.4 37.2 %copy-start.69 = (f32[512]{0:T(512)S(1)}, f32[512]{0:T(512)}, u32[]{:S(2)}) copy-start(f32[512]{0:T(512)} %copy-done.68) | copy-start | bytes 6148
  879.4 39.2 %copy-start.75 = (f32[512]{0:T(512)S(1)}, f32[512]{0:T(512)}, u32[]{:S(2)}) copy-start(f32[512]{0:T(512)} %copy-done.74) | copy-start | bytes 6148
  879.4 39.3 %copy-start.73 = (f32[512]{0:T(512)S(1)}, f32[512]{0:T(512)}, u32[]{:S(2)}) copy-start(f32[512]{0:T(512)} %copy-done.72) | copy-start | bytes 6148
  1193.0 81.9 %copy-start.53 = (f32[2048]{0:T(1024)S(1)}, f32[2048]{0:T(1024)}, u32[]{:S(2)}) copy-start(f32[2048]{0:T(1024)} %copy-done.52) | copy-start | bytes 24580
  1193.0 81.9 %copy-start.59 = (f32[1,1024]{1,0:T(1,128)S(1)}, f32[1,1024]{1,0:T(1,128)}, u32[]{:S(2)}) copy-start(f32[1,1024]{1,0:T(1,128)} %copy-done.58) | copy-start | bytes 12292
  1197.4 83.3 %copy-start.65 = (f32[2048]{0:T(1024)S(1)}, f32[2048]{0:T(1024)}, u32[]{:S(2)}) copy-start(f32[2048]{0:T(1024)} %copy-done.64) | copy-start | bytes 24580
  1197.4 83.3 %copy-start.57 = (f32[2048]{0:T(1024)S(1)}, f32[2048]{0:T(1024)}, u32[]{:S(2)}) copy-start(f32[2048]{0:T(1024)} %copy-done.56) | copy-start | bytes 24580
  (104 other events, 700.6 us)
Sparse Core Ops, SparseCore 0:
  15.6 35.8 all-gather.9
  53.6 104.0 all-gather.7
  226.7 54.3 reduce-scatter.7
  285.2 33.0 all-gather.11
  369.0 54.3 reduce-scatter.9
  428.1 33.0 all-gather.13
  462.8 33.0 all-gather.15
  516.9 31.8 reduce-scatter.13
  551.1 54.3 reduce-scatter.11
  612.8 33.0 all-gather.17
  686.0 31.8 reduce-scatter.15
  727.9 33.0 all-gather.19
  834.0 31.8 reduce-scatter.17
  873.9 298.9 all-reduce.3
  1175.7 99.0 reduce-scatter.19
where the time goes:
time: 1350 us; the launch traced here: 1340 us
  waiting for transfers between devices  786 us (58%)
  matrix products  230 us (17%)
  local copies, waits for them, and re-layouts  137 us (10%)
  other arithmetic  93.8 us (7%)
  blocking collectives  76.1 us (6%)
  between operations  15.2 us (1%)
    psum x1, waiting for transfers between devices, shards(): lax.psum(d_cross_q.astype(jnp.bfloat16), 'dp').astype(jnp.float32)  250 us
    reduce_scatter x3, waiting for transfers between devices, branch_sum(): lax.psum_scatter(term(jnp.int32(0), lax.axis_size('tensor') * own_rows),...  162 us
    all_gather x1, waiting for transfers between devices, shards(): lax.all_gather(in_normed, 'tensor', axis=0, tiled=True)  102 us
    reduce_scatter x1, waiting for transfers between devices, back_inputs(): lax.psum_scatter(term(jnp.int32(0), own_rows * lax.axis_size('tensor')).a...  77.4 us
    dot_general x10, matrix products, matmul(): return jnp.dot(left, right, preferred_element_type=jnp.float32)  66.2 us
    all_gather x2, waiting for transfers between devices, gather_rows(): return lax.all_gather(normed, 'tensor', axis=0, tiled=True)  65.2 us
    all_gather x3, waiting for transfers between devices, gather_grads(): return lax.all_gather(grads, 'tensor', axis=0, tiled=True)  62.9 us
    dot_general x10, matrix products, times_transposed(): lax.dot_general(left, right, (((1,), (1,)), ((), ())), preferred_element_...  58.8 us
  transfers between devices with their start and end apart: 15, of which 14 were waited for; matrix products, arithmetic and copies ran while one was open for 11% of the time, Pallas kernels for 0%

commit v1 on v0

--- a/solution.py
+++ b/solution.py
@@ -352,7 +352,7 @@
         d_upb,
         d_down,
     ) = (
-        lax.psum(d_cross_q.astype(jnp.bfloat16), "dp").astype(jnp.float32),
+        jnp.sum(lax.all_gather(d_cross_q.astype(jnp.bfloat16), "dp"), axis=0).astype(jnp.float32),
         lax.psum(d_cross_k.astype(jnp.bfloat16), "dp").astype(jnp.float32),
         lax.psum(d_cross_v.astype(jnp.bfloat16), "dp").astype(jnp.float32),
         lax.psum(d_cross_o.astype(jnp.bfloat16), "dp").astype(jnp.float32),

time: 1350 us -> 1410 us (1.044)
  waiting for transfers between devices: 786 us -> 835 us
    all_gather x0 -> x1, waiting for transfers between devices: none -> 66.9 us  [shards(): lax.all_gather(d_cross_q.astype(jnp.bfloat16), 'dp')]
    psum x1, waiting for transfers between devices: 250 us -> 227 us  [shards(): lax.psum(d_cross_k.astype(jnp.bfloat16), 'dp').astype(jnp.float32)]
  transfers between devices with their start and end apart: 15 -> 16, of which waited for: 14 -> 15; matrix products, arithmetic and copies ran while one was open for 11% -> 12% of each run, Pallas kernels for 0% -> 0%
where the time goes in v1:
time: 1410 us; the launch traced here: 1400 us
  waiting for transfers between devices  835 us (59%)
  matrix products  231 us (16%)
  local copies, waits for them, and re-layouts  138 us (10%)
  other arithmetic  103 us (7%)
  blocking collectives  78.8 us (6%)
  between operations  14.9 us (1%)
    psum x1, waiting for transfers between devices, shards(): lax.psum(d_cross_k.astype(jnp.bfloat16), 'dp').astype(jnp.float32)  227 us
    reduce_scatter x3, waiting for transfers between devices, branch_sum(): lax.psum_scatter(term(jnp.int32(0), lax.axis_size('tensor') * own_rows),...  162 us
    all_gather x1, waiting for transfers between devices, shards(): lax.all_gather(in_normed, 'tensor', axis=0, tiled=True)  102 us
    reduce_scatter x1, waiting for transfers between devices, back_inputs(): lax.psum_scatter(term(jnp.int32(0), own_rows * lax.axis_size('tensor')).a...  79.5 us
    all_gather x1, waiting for transfers between devices, shards(): lax.all_gather(d_cross_q.astype(jnp.bfloat16), 'dp')  66.9 us
    dot_general x10, matrix products, matmul(): return jnp.dot(left, right, preferred_element_type=jnp.float32)  66.2 us
    all_gather x2, waiting for transfers between devices, gather_rows(): return lax.all_gather(normed, 'tensor', axis=0, tiled=True)  65.5 us
    all_gather x3, waiting for transfers between devices, gather_grads(): return lax.all_gather(grads, 'tensor', axis=0, tiled=True)  62.4 us
  transfers between devices with their start and end apart: 16, of which 15 were waited for; matrix products, arithmetic and copies ran while one was open for 12% of the time, Pallas kernels for 0%

profile of v1, /device:TPU:0, one launch (start us, length us, event | category | flops | bytes accessed | tf_op | source)
XLA Modules:
  0.0 1404.5 jit_solution(5708767779935764720)
XLA Ops:
  24.9 26.5 %all-gather.12.cloned.1.call-done = bf16[1024,1024]{1,0:T(8,128)(2,1)} async-done(((bf16[512,1024]{1,0:T(8,128)(2,1)}), bf16[1024,1024]{1,0:T(8,128)(2,1)}) %all-gather.12.cloned.1.call-update) | async-done | bytes 2097168 | tf_op jit(solution)/shard_map/all_gather | solution.py:234
  56.1 101.5 %all-gather.10.cloned.1.call-done = bf16[4096,1024]{1,0:T(8,128)(2,1)} async-done(((bf16[2048,1024]{1,0:T(8,128)(2,1)}), bf16[4096,1024]{1,0:T(8,128)(2,1)}) %all-gather.10.cloned.1.call-update) | async-done | bytes 8388624 | tf_op jit(solution)/shard_map/all_gather | solution.py:235
  157.6 9.4 convolution_convert_fusion.3
  179.3 9.4 convolution_convert_fusion.4
  196.8 24.9 %while.62 = (s32[]{:T(128)}, bf16[2,4,128,4,128]{4,3,2,1,0:T(4,128)(2,1)}, f32[2,4,4,128]{3,2,1,0:T(4,128)S(1)}, bf16[2,4,512,4,128]{4,3,2,1,0:T(4,128)(2,1)}, s...) while((s32[]{:T(128)}, ...), condition=%wide.region_8.9_spmd, body=%wide.region_5.8_spmd.sunk | while | flops 549715968 | bytes 45163760 | solution.py:97
  227.2 53.8 %reduce-scatter.8.cloned.1.call-done = f32[512,1024]{1,0:T(8,128)} async-done(((f32[1024,1024]{1,0:T(8,128)}), f32[512,1024]{1,0:T(8,128)}) %reduce-scatter.8.cloned.1.call-update) | async-done | bytes 2097168 | tf_op jit(solution)/shard_map/reduce_scatter | solution.py:166
  285.1 33.2 %all-gather.14.cloned.1.call-done = bf16[1024,1024]{1,0:T(8,128)(2,1)} async-done(((bf16[512,1024]{1,0:T(8,128)(2,1)}), bf16[1024,1024]{1,0:T(8,128)(2,1)}) %all-gather.14.cloned.1.call-update) | async-done | bytes 2097168 | tf_op jit(solution)/shard_map/all_gather | solution.py:154
  345.3 18.6 %while.63 = (s32[]{:T(128)}, bf16[2,4,128,4,128]{4,3,2,1,0:T(4,128)(2,1)}, bf16[2,4,128,4,128]{2,4,3,1,0:T(8,128)(2,1)}, bf16[2,4,128,4,128]{4,2,3,1,0:T(8,128)(...) while((s32[]{:T(128)}, bf16[2,4,128,4,128]{4,3,2,1,0:T(4,128)(2,1)}, ...), condition=%wide.region_15.16_spmd, body=%wide.region_12.15_spmd.sunk | while | flops 136053376 | bytes 6309973 | solution.py:97
  368.9 54.5 %reduce-scatter.10.cloned.1.call-done = f32[512,1024]{1,0:T(8,128)} async-done(((f32[1024,1024]{1,0:T(8,128)}), f32[512,1024]{1,0:T(8,128)}) %reduce-scatter.10.cloned.1.call-update) | async-done | bytes 2097168 | tf_op jit(solution)/shard_map/reduce_scatter | solution.py:166
  429.0 32.3 %all-gather.16.cloned.1.call-done = bf16[1024,1024]{1,0:T(8,128)(2,1)} async-done(((bf16[512,1024]{1,0:T(8,128)(2,1)}), bf16[1024,1024]{1,0:T(8,128)(2,1)}) %all-gather.16.cloned.1.call-update) | async-done | bytes 2097168 | tf_op jit(solution)/shard_map/all_gather | solution.py:154
  461.2 10.9 fusion.228
  472.1 23.8 %all-gather.18.cloned.1.call-done = bf16[1024,1024]{1,0:T(8,128)(2,1)} async-done(((bf16[512,1024]{1,0:T(8,128)(2,1)}), bf16[1024,1024]{1,0:T(8,128)(2,1)}) %all-gather.18.cloned.1.call-update) | async-done | bytes 2097168 | tf_op jit(solution)/shard_map/all_gather | solution.py:158
  495.9 13.1 fusion.227
  517.0 11.8 fusion.211
  528.9 19.9 %reduce-scatter.14.cloned.1.call-done = bf16[512,1024]{1,0:T(8,128)(2,1)} async-done(((bf16[1024,1024]{1,0:T(8,128)(2,1)}), bf16[512,1024]{1,0:T(8,128)(2,1)}) %reduce-scatter.14.cloned.1.call-update) | async-done | bytes 1048592 | tf_op jit(solution)/shard_map/reduce_scatter | solution.py:175
  551.4 54.1 %reduce-scatter.12.cloned.1.call-done = f32[512,1024]{1,0:T(8,128)} async-done(((f32[1024,1024]{1,0:T(8,128)}), f32[512,1024]{1,0:T(8,128)}) %reduce-scatter.12.cloned.1.call-update) | async-done | bytes 2097168 | tf_op jit(solution)/shard_map/reduce_scatter | solution.py:166
  614.2 8.9 while.64
  623.1 22.8 %all-gather.20.cloned.1.call-done = bf16[1024,1024]{1,0:T(8,128)(2,1)} async-done(((bf16[512,1024]{1,0:T(8,128)(2,1)}), bf16[1024,1024]{1,0:T(8,128)(2,1)}) %all-gather.20.cloned.1.call-update) | async-done | bytes 2097168 | tf_op jit(solution)/shard_map/all_gather | solution.py:158
  655.9 22.7 %while.65 = (s32[]{:T(128)}, bf16[2,4,128,4,128]{4,3,2,1,0:T(4,128)(2,1)}, bf16[2,4,128,4,128]{4,3,2,1,0:T(4,128)(2,1)}, bf16[2,4,128,4,128]{4,3,2,1,0:T(4,128)(...) while((s32[]{:T(128)}, ...), condition=%wide.region_29.30_spmd, body=%wide.region_27.29_spmd.sunk | while | flops 339212800 | bytes 40413460 | solution.py:145
  686.4 9.5 convolution_convert_fusion.6
  695.9 22.0 %reduce-scatter.16.cloned.1.call-done = bf16[512,1024]{1,0:T(8,128)(2,1)} async-done(((bf16[1024,1024]{1,0:T(8,128)(2,1)}), bf16[512,1024]{1,0:T(8,128)(2,1)}) %reduce-scatter.16.cloned.1.call-update) | async-done | bytes 1048592 | tf_op jit(solution)/shard_map/reduce_scatter | solution.py:175
  727.9 12.6 convolution_convert_fusion.5
  745.1 15.9 %all-gather.22.cloned.1.call-done = bf16[1024,1024]{1,0:T(8,128)(2,1)} async-done(((bf16[512,1024]{1,0:T(8,128)(2,1)}), bf16[1024,1024]{1,0:T(8,128)(2,1)}) %all-gather.22.cloned.1.call-update) | async-done | bytes 2097168 | tf_op jit(solution)/shard_map/all_gather | solution.py:158
  765.5 64.1 %while.66 = (s32[]{:T(128)}, bf16[2,4,128,4,128]{4,3,2,1,0:T(4,128)(2,1)}, bf16[2,4,512,4,128]{4,3,2,1,0:T(4,128)(2,1)}, bf16[2,4,512,4,128]{4,3,2,1,0:T(4,128)(...) while((s32[]{:T(128)}, ...), condition=%wide.region_35.36_spmd, body=%wide.region_33.35_spmd.sunk | while | flops 1361575936 | bytes 150537648 | solution.py:145
  857.9 10.5 fusion.142
  868.4 11.7 add_convert_fusion
  885.3 34.9 %psum.102 = bf16[2048]{0:T(1024)(128)(2,1)S(1)} all-reduce(bf16[2048]{0:T(1024)(128)(2,1)S(1)} %copy-done.78), channel_id=1, replica_groups=mesh['dp'=16,'tensor'=2] {'dp'}, use_global_device_ids=true, to_apply=%region_66.67 | all-reduce | flops 2048 | bytes 8192 | tf_op jit(solution)/shard_map/psum | solution.py:364
  927.6 227.3 %all-reduce.4.cloned.1.call-done = (bf16[1024,512]{1,0:T(8,128)(2,1)}, bf16[1024,512]{1,0:T(8,128)(2,1)}, bf16[512,1024]{1,0:T(8,128)(2,1)}, bf16[1024,512]{1,0:...) async-done(((bf16[1024,512]{1,0:T(8,128)(2,1)}, ...) | async-done | bytes 15728656 | tf_op jit(solution)/shard_map/psum | solution.py:356
  1177.7 79.5 %reduce-scatter.20.cloned.1.call-done = bf16[2048,1024]{1,0:T(8,128)(2,1)} async-done(((bf16[4096,1024]{1,0:T(8,128)(2,1)}), bf16[2048,1024]{1,0:T(8,128)(2,1)}) %reduce-scatter.20.cloned.1.call-update) | async-done | bytes 4194320 | tf_op jit(solution)/shard_map/reduce_scatter | solution.py:184
  1268.6 43.9 %all-reduce = (f32[4,1024]{1,0:T(4,128)}, f32[4,1024]{1,0:T(4,128)}, f32[3,1024]{1,0:T(4,128)}) all-reduce(f32[4,1024]{1,0:T(4,128)S(1)} %get-tuple-element.480, f32[4,1024]{1,0:T(4,128)S(1)} %get-tuple-element.481, f32[3,1024]{1,0:T(4,128)S(1)} %pad_maximum_fusion.2), channel_id=1, replica_groups=mesh['dp'=16,'tensor'=2] {'dp','tensor'}, use_global_device_ids=true, to_apply=%region_46.47 | all-reduce | flops 11264 | bytes 90112 | tf_op jit(solution)/shard_map/psum | solution.py:339
  1320.4 66.9 %all-gather.24.cloned.1.call-done = bf16[16384,512]{1,0:T(8,128)(2,1)} async-done(((bf16[1024,512]{1,0:T(8,128)(2,1)}), bf16[16384,512]{1,0:T(8,128)(2,1)}) %all-gather.24.cloned.1.call-update) | async-done | bytes 16777232 | tf_op jit(solution)/shard_map/all_gather | solution.py:355
  1387.3 8.9 reduce_sum.370
  (466 shorter events, 368.6 us)
Async XLA Ops:
  7.2 150.5 %copy-start = (bf16[1024,512]{1,0:T(8,128)(2,1)S(1)}, bf16[1024,512]{1,0:T(8,128)(2,1)}, u32[]{:S(2)}) copy-start(bf16[1024,512]{1,0:T(8,128)(2,1)} %param.36) | copy-start | bytes 3145732
  7.2 44.2 %all-gather.12.cloned.1.call-start = ((), (), s32[]{:S(2)}) async-start(), calls=%async_computation.8 | async-start | bytes 3145728 | tf_op jit(solution)/shard_map/all_gather | solution.py:234
  15.5 142.1 %all-gather.10.cloned.1.call-start = ((), (), s32[]{:S(2)}) async-start(), calls=%async_computation.7 | async-start | bytes 12582912 | tf_op jit(solution)/shard_map/all_gather | solution.py:235
  24.0 27.5 %copy-start.86 = (bf16[1024,512]{1,0:T(8,128)(2,1)S(1)}, bf16[1024,512]{1,0:T(8,128)(2,1)}, u32[]{:S(2)}) copy-start(bf16[1024,512]{1,0:T(8,128)(2,1)} %param.35) | copy-start | bytes 3145732
  24.0 257.0 %reduce-scatter.8.cloned.1.call-start = ((), (), s32[]{:S(2)}) async-start(), calls=%async_computation.9 | async-start | bytes 6291456 | tf_op jit(solution)/shard_map/reduce_scatter | solution.py:166
  226.5 91.8 %all-gather.14.cloned.1.call-start = ((), (), s32[]{:S(2)}) async-start(), calls=%async_computation.10 | async-start | bytes 3145728 | tf_op jit(solution)/shard_map/all_gather | solution.py:154
  283.3 140.1 %copy-start.8 = (f32[512,1024]{1,0:T(8,128)}, f32[512,1024]{1,0:T(8,128)S(1)}, u32[]{:S(2)}) copy-start(f32[512,1024]{1,0:T(8,128)S(1)} %get-tuple-element.450) | copy-start | bytes 6291460
  285.1 138.3 %reduce-scatter.10.cloned.1.call-start = ((), (), s32[]{:S(2)}) async-start(), calls=%async_computation.11 | async-start | bytes 6291456 | tf_op jit(solution)/shard_map/reduce_scatter | solution.py:166
  368.8 92.4 %all-gather.16.cloned.1.call-start = ((), (), s32[]{:S(2)}) async-start(), calls=%async_computation.12 | async-start | bytes 3145728 | tf_op jit(solution)/shard_map/all_gather | solution.py:154
  428.0 67.9 %all-gather.18.cloned.1.call-start = ((), (), s32[]{:S(2)}) async-start(), calls=%async_computation.14 | async-start | bytes 3145728 | tf_op jit(solution)/shard_map/all_gather | solution.py:158
  428.7 120.0 %reduce-scatter.14.cloned.1.call-start = ((), (), s32[]{:S(2)}) async-start(), calls=%async_computation.15 | async-start | bytes 3145728 | tf_op jit(solution)/shard_map/reduce_scatter | solution.py:175
  516.7 88.8 %reduce-scatter.12.cloned.1.call-start = ((), (), s32[]{:S(2)}) async-start(), calls=%async_computation.13 | async-start | bytes 6291456 | tf_op jit(solution)/shard_map/reduce_scatter | solution.py:166
  528.8 117.1 %all-gather.20.cloned.1.call-start = ((), (), s32[]{:S(2)}) async-start(), calls=%async_computation.16 | async-start | bytes 3145728 | tf_op jit(solution)/shard_map/all_gather | solution.py:158
  612.6 105.3 %reduce-scatter.16.cloned.1.call-start = ((), (), s32[]{:S(2)}) async-start(), calls=%async_computation.17 | async-start | bytes 3145728 | tf_op jit(solution)/shard_map/reduce_scatter | solution.py:175
  685.8 75.1 %all-gather.22.cloned.1.call-start = ((), (), s32[]{:S(2)}) async-start(), calls=%async_computation.18 | async-start | bytes 3145728 | tf_op jit(solution)/shard_map/all_gather | solution.py:158
  686.4 31.5 %copy-start.9 = (f32[512,1024]{1,0:T(8,128)S(1)}, f32[512,1024]{1,0:T(8,128)}, u32[]{:S(2)}) copy-start(f32[512,1024]{1,0:T(8,128)} %copy-done.8) | copy-start | bytes 6291460
  727.7 193.2 %reduce-scatter.18.cloned.1.call-start = ((), (), s32[]{:S(2)}) async-start(), calls=%async_computation.19 | async-start | bytes 3145728 | tf_op jit(solution)/shard_map/reduce_scatter | solution.py:175
  833.9 321.0 %all-reduce.4.cloned.1.call-start = ((), (), s32[]{:S(2)}) async-start(), calls=%async_computation.22 | async-start | bytes 31457280 | tf_op jit(solution)/shard_map/psum | solution.py:356
  857.8 399.3 %reduce-scatter.20.cloned.1.call-start = ((), (), s32[]{:S(2)}) async-start(), calls=%async_computation.20 | async-start | bytes 12582912 | tf_op jit(solution)/shard_map/reduce_scatter | solution.py:184
  880.1 40.6 %copy-start.73 = (f32[1024]{0:T(1024)S(1)}, f32[1024]{0:T(1024)}, u32[]{:S(2)}) copy-start(f32[1024]{0:T(1024)} %get-tuple-element.443) | copy-start | bytes 12292
  880.1 40.6 %copy-start.74 = (f32[1024]{0:T(1024)S(1)}, f32[1024]{0:T(1024)}, u32[]{:S(2)}) copy-start(f32[1024]{0:T(1024)} %get-tuple-element.350) | copy-start | bytes 12292
  880.2 40.6 %copy-start.75 = (f32[1024]{0:T(1024)S(1)}, f32[1024]{0:T(1024)}, u32[]{:S(2)}) copy-start(f32[1024]{0:T(1024)} %get-tuple-element.351) | copy-start | bytes 12292
  880.2 40.7 %copy-start.16 = (bf16[512,1024]{1,0:T(8,128)(2,1)S(1)}, bf16[512,1024]{1,0:T(8,128)(2,1)}, u32[]{:S(2)}) copy-start(bf16[512,1024]{1,0:T(8,128)(2,1)} %param.29) | copy-start | bytes 3145732
  880.2 40.7 %copy-start.60 = (f32[1,1024]{1,0:T(1,128)S(1)}, f32[1,1024]{1,0:T(1,128)}, u32[]{:S(2)}) copy-start(f32[1,1024]{1,0:T(1,128)} %copy-done.59) | copy-start | bytes 12292
  880.2 40.7 %copy-start.64 = (f32[512]{0:T(512)S(1)}, f32[512]{0:T(512)}, u32[]{:S(2)}) copy-start(f32[512]{0:T(512)} %copy-done.63) | copy-start | bytes 6148
  880.2 42.8 %copy-start.68 = (f32[512]{0:T(512)S(1)}, f32[512]{0:T(512)}, u32[]{:S(2)}) copy-start(f32[512]{0:T(512)} %copy-done.67) | copy-start | bytes 6148
  880.2 42.8 %copy-start.66 = (f32[512]{0:T(512)S(1)}, f32[512]{0:T(512)}, u32[]{:S(2)}) copy-start(f32[512]{0:T(512)} %copy-done.65) | copy-start | bytes 6148
  880.2 507.1 %all-gather.24.cloned.1.call-start = ((), (), s32[]{:S(2)}) async-start(), calls=%async_computation.21 | async-start | bytes 17825792 | tf_op jit(solution)/shard_map/all_gather | solution.py:355
  1173.2 83.9 %copy-start.52 = (f32[2048]{0:T(1024)S(1)}, f32[2048]{0:T(1024)}, u32[]{:S(2)}) copy-start(f32[2048]{0:T(1024)} %copy-done.51) | copy-start | bytes 24580
  1173.2 83.9 %copy-start.58 = (f32[1,1024]{1,0:T(1,128)S(1)}, f32[1,1024]{1,0:T(1,128)}, u32[]{:S(2)}) copy-start(f32[1,1024]{1,0:T(1,128)} %copy-done.57) | copy-start | bytes 12292
  1177.7 85.3 %copy-start.62 = (f32[2048]{0:T(1024)S(1)}, f32[2048]{0:T(1024)}, u32[]{:S(2)}) copy-start(f32[2048]{0:T(1024)} %copy-done.61) | copy-start | bytes 24580
  1177.7 85.3 %copy-start.56 = (f32[2048]{0:T(1024)S(1)}, f32[2048]{0:T(1024)}, u32[]{:S(2)}) copy-start(f32[2048]{0:T(1024)} %copy-done.55) | copy-start | bytes 24580
  (96 other events, 469.1 us)
Sparse Core Ops, SparseCore 0:
  15.6 35.8 all-gather.11
  53.6 104.0 all-gather.9
  226.7 54.3 reduce-scatter.7
  285.2 33.0 all-gather.13
  368.9 54.3 reduce-scatter.9
  428.1 33.0 all-gather.15
  462.8 33.0 all-gather.17
  516.8 31.8 reduce-scatter.13
  551.1 54.3 reduce-scatter.11
  612.8 33.0 all-gather.19
  686.0 31.8 reduce-scatter.15
  727.8 33.0 all-gather.21
  834.0 31.8 reduce-scatter.17
  873.6 281.2 all-reduce.3
  1157.6 99.5 reduce-scatter.19
  1259.8 127.4 all-gather.23
